TPU v7x, 32 devices: a whole 2x2x4 slice. The times are simulated.
32 devices in a mesh: grp: 2 (over x), beam: 16 (over z, y, core).
Axes of the slice: x: 2, y: 2, z: 4, core: 2. Of those that a mesh axis runs over, the one named last changes fastest.
Arguments:
- s_matrix: bfloat16 [2, 2048, 16, 4096], P(None, ('grp', 'beam')), parts along dimension 1, may hold values from -6 to 6
- beam_weight: float32 [2, 2048], P(None, ('grp', 'beam')), parts along dimension 1, may hold values from -0.25 to 0.25
- probe_shift: int32 [256, 2], P(('grp', 'beam')), parts along dimension 0, may hold values from 0 to 191
- probe_cutoff: int32 [256], P(('grp', 'beam')), parts along dimension 0, may hold values from 64 to 512
- target: bfloat16 [2, 256, 4096], P(None, ('grp', 'beam')), parts along dimension 1, may hold values from -3 to 3
- target_exp: int32 [256], P(('grp', 'beam')), parts along dimension 0, may hold values from -1 to 2
Outputs:
- s_grad: bfloat16 [2, 2048, 16, 4096], P(None, ('grp', 'beam')), parts along dimension 1
There are 2 independent parts, one for each index of `grp`. A program takes and returns all parts, laid end to end along the dimension named above; each array names one. Nothing has to cross between parts.
All inputs are finite; a program needn't handle non-finite values.
Results may differ from a plain program's by a relative error of at most 0.006.
Values may be sent and summed in bfloat16 or wider, within the bound.
A program may use at most 128 MiB of HBM per device.

v0:
```python
import math

import jax
import jax.numpy as jnp
from jax import lax
from jax.sharding import PartitionSpec as P

SIDE = 32
GRID = 192
TILE_SIDE = 4


TWO_PI = 2.0 * math.pi


def window_of(shift):
    step = GRID // TILE_SIDE
    return shift[:, 0] // step * TILE_SIDE + shift[:, 1] // step


def coefficients(beam_index, weight, shift, cutoff):
    half = SIDE // 2
    freq_x = beam_index % SIDE - half
    freq_y = beam_index // SIDE - half
    ramp = (freq_x[None, :] * shift[:, 0:1] + freq_y[None, :] * shift[:, 1:2]) % GRID
    phase = ramp.astype(jnp.float32) * (TWO_PI / GRID)
    inside = (freq_x * freq_x + freq_y * freq_y)[None, :] <= cutoff[:, None]
    cosine = jnp.cos(phase)
    sine = jnp.sin(phase)
    w_real = weight[0][None, :]
    w_imag = weight[1][None, :]
    c_real = jnp.where(inside, w_real * cosine + w_imag * sine, 0.0)
    c_imag = jnp.where(inside, w_imag * cosine - w_real * sine, 0.0)
    return (c_real.astype(jnp.bfloat16), c_imag.astype(jnp.bfloat16))


def body(s_matrix, beam_weight, probe_shift, probe_cutoff, target, target_exp):
    local = s_matrix.shape[1]
    tile_count = s_matrix.shape[2]
    pixels = s_matrix.shape[3]
    beam_index = lax.axis_index("beam") * local + jnp.arange(local, dtype=jnp.int32)
    shifts, cutoffs, exponents = (
        lax.all_gather(probe_shift, "beam", axis=0, tiled=True),
        lax.all_gather(probe_cutoff, "beam", axis=0, tiled=True),
        lax.all_gather(target_exp, "beam", axis=0, tiled=True),
    )
    total = shifts.shape[0]
    c_real, c_imag = coefficients(beam_index, beam_weight, shifts, cutoffs)
    windows = window_of(shifts)
    onehot = windows[:, None] == jnp.arange(tile_count, dtype=jnp.int32)[None, :]
    zero = jnp.zeros((), jnp.bfloat16)
    width = local * tile_count
    e_real = jnp.where(onehot[:, None, :], c_real[:, :, None], zero).reshape(total, width)
    e_imag = jnp.where(onehot[:, None, :], c_imag[:, :, None], zero).reshape(total, width)
    s_flat = s_matrix.reshape(2 * width, pixels)
    left_re = jnp.concatenate([e_real, -e_imag], axis=1)
    left_im = jnp.concatenate([e_imag, e_real], axis=1)
    wave_re = jnp.dot(left_re, s_flat, preferred_element_type=jnp.float32)
    wave_im = jnp.dot(left_im, s_flat, preferred_element_type=jnp.float32)
    whole_targets = lax.all_gather(target, "beam", axis=1, tiled=True)
    full_re, full_im = lax.psum((wave_re, wave_im), "beam")
    scale = jnp.exp2(exponents.astype(jnp.float32))[None, :, None]
    residual = (jnp.stack([full_re, full_im]) - whole_targets.astype(jnp.float32) * scale).astype(
        jnp.bfloat16
    )
    stacked_coef = jnp.concatenate([e_real, e_imag], axis=0)
    flipped_coef = jnp.concatenate([e_real, -e_imag], axis=0)
    res_direct = jnp.concatenate([residual[0], residual[1]], axis=0)
    res_swapped = jnp.concatenate([residual[1], residual[0]], axis=0)
    dims = (((0,), (0,)), ((), ()))
    g_re = lax.dot_general(stacked_coef, res_direct, dims, preferred_element_type=jnp.float32)
    g_im = lax.dot_general(flipped_coef, res_swapped, dims, preferred_element_type=jnp.float32)
    s_grad = jnp.stack([g_re, g_im]).reshape(2, local, tile_count, pixels)
    return s_grad.astype(jnp.bfloat16)


def solution(mesh):
    return jax.shard_map(
        body,
        mesh=mesh,
        in_specs=(
            P(None, ("grp", "beam"), None, None),
            P(None, ("grp", "beam")),
            P(("grp", "beam"), None),
            P(("grp", "beam")),
            P(None, ("grp", "beam"), None),
            P(("grp", "beam")),
        ),
        out_specs=P(None, ("grp", "beam"), None, None),
        check_vma=False,
    )
```

profile of v0, /device:TPU:0, one launch (start us, length us, event | category | flops | bytes accessed | tf_op | source)
XLA Modules:
  0.0 235.2 jit_solution(14886051234407672063)
XLA Ops:
  6.5 0.0 all-reduce.6.cloned.1.call-start
  6.6 0.8 slice_bitcast_fusion.3
  7.3 23.4 %all-gather = s32[16,8,2]{1,2,0:T(2,128)S(1)} all-gather(s32[1,8,2]{1,2,0:T(2,128)} %bitcast.40), channel_id=1, replica_groups=mesh['grp'=2,'beam'=16] {'beam'}, dimensions={0}, use_global_device_ids=true | all-gather | bytes 1088 | tf_op jit(solution)/shard_map/all_gather | solution.py:43
  30.7 0.1 reshape.326
  30.8 1.2 dynamic-slice
  32.8 0.9 dynamic-update-slice
  33.6 0.8 dynamic-update-slice.1
  34.5 7.2 %all-reduce.2 = (s32[128]{0:T(128)S(1)}, s32[128]{0:T(128)S(1)}) all-reduce(s32[128]{0:T(128)S(1)} %dynamic-update-slice, s32[128]{0:T(128)S(1)} %dynamic-update-slice.1), channel_id=1, replica_groups=mesh['grp'=2,'beam'=16] {'beam'}, use_global_device_ids=true, to_apply=%add | all-reduce | flops 256 | bytes 2048
  41.6 0.2 fusion.16
  41.9 0.1 broadcast_select_fusion
  41.9 0.1 bitcast_negate_fusion
  42.0 0.0 copy-start
  42.0 9.6 %convolution_bitcast_fusion.1 = f32[1,128,4096]{2,1,0:T(8,128)} fusion(bf16[2048,4096]{1,0:T(8,128)(2,1)} %bitcast.30, bf16[128,1024]{0,1:T(8,128)(2,1)S(1)} %bitcast_negate_fusion, bf16[128,1024]{0,1:T(8,128)(2,1)S(1)} %bitcast.34), kind=kOutput, calls=%fused_computation.4 | convolution fusion | flops 2148532224 | bytes 19398656 | tf_op jit(solution)/shard_map/dot_general | solution.py:58
  51.6 1.7 copy-done
  53.3 3.7 %convolution_bitcast_fusion = f32[1,128,4096]{2,1,0:T(8,128)} fusion(bf16[2048,4096]{1,0:T(8,128)(2,1)S(1)} %bitcast.31, bf16[128,1024]{0,1:T(8,128)(2,1)S(1)} %bitcast.35, bf16[128,1024]{0,1:T(8,128)(2,1)S(1)} %bitcast.38), kind=kOutput, calls=%fused_computation.3 | convolution fusion | flops 2148532224 | bytes 19398656 | tf_op jit(solution)/shard_map/dot_general | solution.py:59
  57.0 0.0 all-reduce.6.cloned.1.call-update
  57.0 0.2 all-gather.3.cloned.1.call-start
  57.2 0.5 all-gather.3.cloned.1.call-update
  57.8 112.7 %all-reduce.6.cloned.1.call-done = (f32[1,128,4096]{2,1,0:T(8,128)}, f32[1,128,4096]{2,1,0:T(8,128)}) async-done(((f32[1,128,4096]{2,1,0:T(8,128)}, f32[1,128,4096]{2,1,0:T(8,128)}), (f32[1,128,4096]{2,1,0:T(8,128)}, f32[1,128,4096]{2,1,0:T(8,128)})) %all-reduce.6.cloned.1.call-update) | async-done | bytes 4194320 | tf_op jit(solution)/shard_map/psum | solution.py:61
  170.5 42.7 %all-gather.3.cloned.1.call-done = bf16[2,128,4096]{2,1,0:T(8,128)(2,1)} async-done(((bf16[2,8,4096]{2,1,0:T(8,128)(2,1)}), bf16[2,128,4096]{2,1,0:T(8,128)(2,1)}) %all-gather.3.cloned.1.call-update) | async-done | bytes 2097168 | tf_op jit(solution)/shard_map/all_gather | solution.py:60
  213.2 3.6 %fusion = bf16[2,128,4096]{2,1,0:T(8,128)(2,1)S(1)} fusion(f32[1,128,4096]{2,1,0:T(8,128)} %get-tuple-element.7, f32[1,128,4096]{2,1,0:T(8,128)} %get-tuple-element.8, bf16[2,128,4096]{2,1,0:T(8,128)(2,1)} %all-gather.3.cloned.1.call-done, f32[128]{0:T(128)S(1)} %multiply_exponential_fusion), kind=kLoop, calls=%fused_computation.6 | loop fusion | flops 5242880 | bytes 8389120 | tf_op jit(solution)/shard_map/convert_element_type | solution.py:63
  216.8 0.1 slice_bitcast_fusion
  216.9 2.4 convolution_convert_fusion
  219.3 2.4 convolution_convert_fusion.1
  221.6 6.8 %pad_maximum_fusion = bf16[2,64,16,4096]{3,2,1,0:T(8,128)(2,1)} fusion(bf16[1,64,16,4096]{3,2,1,0:T(8,128)(2,1)S(1)} %bitcast.32, bf16[1,64,16,4096]{3,2,1,0:T(8,128)(2,1)S(1)} %bitcast.33), kind=kLoop, calls=%fused_computation | loop fusion | flops 8388608 | bytes 33554432 | tf_op jit(solution)/shard_map/stack | solution.py:73
  (8 shorter events, 0.1 us)
Async XLA Ops:
  6.5 163.9 %all-reduce.6.cloned.1.call-start = ((), (), s32[]{:S(2)}) async-start(), calls=%async_computation.1 | async-start | bytes 8388608 | tf_op jit(solution)/shard_map/psum | solution.py:61
  42.0 11.3 %copy-start = (bf16[2,64,16,4096]{3,2,1,0:T(8,128)(2,1)S(1)}, bf16[2,64,16,4096]{3,2,1,0:T(8,128)(2,1)}, u32[]{:S(2)}) copy-start(bf16[2,64,16,4096]{3,2,1,0:T(8,128)(2,1)} %param.6) | copy-start | bytes 50331652
  57.0 156.1 %all-gather.3.cloned.1.call-start = ((), (), s32[]{:S(2)}) async-start(), calls=%async_computation | async-start | bytes 2228224 | tf_op jit(solution)/shard_map/all_gather | solution.py:60
Sparse Core Ops, SparseCore 0:
  57.1 113.2 all-reduce.5
  172.6 40.4 all-gather.2
where the time goes:
time: 235 us
  waiting for transfers between devices  156 us (66%)
  blocking collectives  30.6 us (13%)
  matrix products  18 us (8%)
  between operations  14.2 us (6%)
  other arithmetic  10.8 us (5%)
  local copies, waits for them, and re-layouts  5.6 us (2%)
    psum x1, waiting for transfers between devices, body(): full_re, full_im = lax.psum((wave_re, wave_im), 'beam')  113 us
    all_gather x1, waiting for transfers between devices, body(): whole_targets = lax.all_gather(target, 'beam', axis=1, tiled=True)  42.7 us
    all_gather x1, blocking collectives, body(): lax.all_gather(probe_shift, 'beam', axis=0, tiled=True)  23.4 us
    dot_general x1, matrix products, body(): wave_re = jnp.dot(left_re, s_flat, preferred_element_type=jnp.float32)  9.63 us
    unnamed x1, blocking collectives  7.17 us
    another operation x1, other arithmetic, body(): s_grad = jnp.stack([g_re, g_im]).reshape(2, local, tile_count, pixels)  6.75 us
  transfers between devices with their start and end apart: 2, of which 2 were waited for; matrix products, arithmetic and copies ran while one was open for 0% of the time, Pallas kernels for 0%

commit v1 on v0

v1 whole, which is shorter than its diff:
```python
import functools
import math

import jax
import jax.numpy as jnp
from jax import lax
from jax.experimental import pallas as pl
from jax.experimental.pallas import tpu as pltpu
from jax.sharding import PartitionSpec as P

SIDE = 32
GRID = 192
TILE_SIDE = 4
TWO_PI = 2.0 * math.pi
CHUNKS = 4
MATMUL_COLUMNS = 512


def stage_strides(n):
    return [2**k for k in range(n.bit_length() - 1)]


def place(me, strides, unit, upto):
    levels = len(strides)
    base = 0
    for k in range(upto):
        base = base + (me // strides[k]) % 2 * (unit * 2 ** (levels - 1 - k))
    return base


def wave_kernel(
    n, local, tile_count, pixels, strides,
    par_ref, weight_ref, target_ref, s_ref,
    res_ref, left_ref,
    pars, s_vmem, acc, sbuf, rbuf,
    par_send, par_recv, s_sem, send_sem, recv_sem,
):
    levels = len(strides)
    me = lax.axis_index("beam")
    unit = par_ref.shape[0]
    rows = n * unit
    width = local * tile_count
    wide = pixels // CHUNKS

    def partner(k):
        return me + (1 - 2 * ((me // strides[k]) % 2)) * strides[k]

    def columns(c):
        return pl.ds(c * wide, wide)

    loads = []
    for c in range(CHUNKS):
        load = pltpu.make_async_copy(s_ref.at[:, columns(c)], s_vmem.at[:, columns(c)], s_sem.at[c])
        load.start()
        loads.append(load)

    barrier = pltpu.get_barrier_semaphore()
    for k in range(levels):
        pl.semaphore_signal(barrier, inc=1, device_id={"beam": partner(k)}, device_id_type=pl.DeviceIdType.MESH)
    pl.semaphore_wait(barrier, levels)

    sent = []

    def send(source, target, send_semaphore, recv_semaphore, k):
        copy = pltpu.make_async_remote_copy(
            src_ref=source,
            dst_ref=target,
            send_sem=send_semaphore,
            recv_sem=recv_semaphore,
            device_id={"beam": partner(k)},
            device_id_type=pl.DeviceIdType.MESH,
        )
        copy.start()
        sent.append(copy)
        return copy

    def mine(k):
        size = unit * 2 ** (levels - k)
        return pl.ds(pl.multiple_of(place(me, strides, unit, k), size), size)

    pars[mine(levels), :] = par_ref[...]
    for k in reversed(range(levels)):
        held = pars.at[mine(k + 1), :]
        send(held, held, par_send.at[k], par_recv.at[k], k).wait_recv()

    half = SIDE // 2
    beam = me * local + lax.broadcasted_iota(jnp.int32, (1, local), 1)
    freq_x = beam % SIDE - half
    freq_y = beam // SIDE - half
    shift_x = pars[:, 0:1]
    shift_y = pars[:, 1:2]
    cutoff = pars[:, 2:3]
    ramp = (freq_x * shift_x + freq_y * shift_y) % GRID
    phase = ramp.astype(jnp.float32) * (TWO_PI / GRID)
    inside = (freq_x * freq_x + freq_y * freq_y) <= cutoff
    cosine = jnp.cos(phase)
    sine = jnp.sin(phase)
    w_real = weight_ref[0:1, :]
    w_imag = weight_ref[1:2, :]
    c_real = jnp.where(inside, w_real * cosine + w_imag * sine, 0.0)
    c_imag = jnp.where(inside, w_imag * cosine - w_real * sine, 0.0)
    is_real = lax.broadcasted_iota(jnp.int32, (rows, 1), 0) % unit < unit // 2
    first = jnp.where(is_real, c_real, c_imag).astype(jnp.bfloat16)
    second = jnp.where(is_real, -c_imag, c_real).astype(jnp.bfloat16)
    step = GRID // TILE_SIDE
    window = shift_x // step * TILE_SIDE + shift_y // step
    place_of = lax.broadcasted_iota(jnp.int32, (1, width), 1)
    chosen = window == place_of % tile_count
    spread = lax.broadcasted_iota(jnp.int32, (local, width), 1) // tile_count
    spread = (spread == lax.broadcasted_iota(jnp.int32, (local, width), 0)).astype(jnp.float32).astype(jnp.bfloat16)
    for at, part in ((0, first), (width, second)):
        full = jnp.dot(part, spread, preferred_element_type=jnp.float32)
        left_ref[:, at : at + width] = jnp.where(chosen, full, 0.0).astype(jnp.bfloat16)

    narrow = min(MATMUL_COLUMNS, wide)

    def multiply(c):
        def tile(i, carry):
            at = pl.ds(pl.multiple_of(c * wide + i * narrow, narrow), narrow)
            acc[:, at] = jnp.dot(left_ref[...], s_vmem[:, at], preferred_element_type=jnp.float32)
            return carry

        lax.fori_loop(0, wide // narrow, tile, 0)

    def scatter_rows(k):
        size = rows // 2 ** (k + 1)
        base = place(me, strides, unit, k)
        bit = (me // strides[k]) % 2
        keep = pl.ds(pl.multiple_of(base + bit * size, size), size)
        give = pl.ds(pl.multiple_of(base + (1 - bit) * size, size), size)
        slot = pl.ds(rows - 2 * size, size)
        return keep, give, slot

    def start_scatter(c, k):
        _, give, slot = scatter_rows(k)
        sbuf[slot, columns(c)] = acc[give, columns(c)].astype(jnp.bfloat16)
        return send(
            sbuf.at[slot, columns(c)], rbuf.at[slot, columns(c)], send_sem.at[c, k], recv_sem.at[c, k], k
        )

    def end_scatter(c, k):
        keep, _, slot = scatter_rows(k)
        acc[keep, columns(c)] += rbuf[slot, columns(c)].astype(jnp.float32)

    def residual(c):
        own = mine(levels)
        scale = jnp.exp2(par_ref[:, 3:4].astype(jnp.float32))
        goal = target_ref[:, columns(c)].astype(jnp.float32) * scale
        res_ref[own, columns(c)] = (acc[own, columns(c)] - goal).astype(jnp.bfloat16)

    def start_gather(c, k):
        held = res_ref.at[mine(k + 1), columns(c)]
        at = 2 * levels - 1 - k
        return send(held, held, send_sem.at[c, at], recv_sem.at[c, at], k)

    flight = {}
    for time in range(CHUNKS + 2 * levels):
        for c in range(CHUNKS):
            at = time - c
            if at < 0 or at > 2 * levels:
                continue
            if at == 0:
                loads[c].wait()
                multiply(c)
            else:
                flight[c].wait_recv()
                if at <= levels:
                    end_scatter(c, at - 1)
            if at < levels:
                flight[c] = start_scatter(c, at)
            elif at < 2 * levels:
                if at == levels:
                    residual(c)
                flight[c] = start_gather(c, 2 * levels - 1 - at)
    for copy in sent:
        copy.wait_send()


def body(n, s_matrix, beam_weight, probe_shift, probe_cutoff, target, target_exp):
    _, local, tile_count, pixels = s_matrix.shape
    probes = probe_shift.shape[0]
    strides = stage_strides(n)
    levels = len(strides)
    unit = 2 * probes
    rows = n * unit
    width = local * tile_count
    pars = jnp.concatenate([probe_shift, probe_cutoff[:, None], target_exp[:, None]], axis=1)
    pars = jnp.pad(jnp.concatenate([pars, pars], axis=0), ((0, 0), (0, 124)))
    vmem = pl.BlockSpec(memory_space=pltpu.VMEM)
    res, left = pl.pallas_call(
        functools.partial(wave_kernel, n, local, tile_count, pixels, strides),
        out_shape=(
            jax.ShapeDtypeStruct((rows, pixels), jnp.bfloat16),
            jax.ShapeDtypeStruct((rows, 2 * width), jnp.bfloat16),
        ),
        in_specs=[vmem, vmem, vmem, pl.BlockSpec(memory_space=pl.ANY)],
        out_specs=(vmem, vmem),
        scratch_shapes=[
            pltpu.VMEM((rows, 128), jnp.int32),
            pltpu.VMEM((2 * width, pixels), jnp.bfloat16),
            pltpu.VMEM((rows, pixels), jnp.float32),
            pltpu.VMEM((rows, pixels), jnp.bfloat16),
            pltpu.VMEM((rows, pixels), jnp.bfloat16),
            pltpu.SemaphoreType.DMA((levels,)),
            pltpu.SemaphoreType.DMA((levels,)),
            pltpu.SemaphoreType.DMA((CHUNKS,)),
            pltpu.SemaphoreType.DMA((CHUNKS, 2 * levels)),
            pltpu.SemaphoreType.DMA((CHUNKS, 2 * levels)),
        ],
        compiler_params=pltpu.CompilerParams(
            collective_id=0, has_side_effects=True, vmem_limit_bytes=60 * 2**20
        ),
    )(pars, beam_weight, target.reshape(unit, pixels), s_matrix.reshape(2 * width, pixels))
    grad = lax.dot_general(left, res, (((0,), (0,)), ((), ())), preferred_element_type=jnp.float32)
    return grad.astype(jnp.bfloat16).reshape(2, local, tile_count, pixels)


def solution(mesh):
    return jax.shard_map(
        functools.partial(body, mesh.shape["beam"]),
        mesh=mesh,
        in_specs=(
            P(None, ("grp", "beam"), None, None),
            P(None, ("grp", "beam")),
            P(("grp", "beam"), None),
            P(("grp", "beam")),
            P(None, ("grp", "beam"), None),
            P(("grp", "beam")),
        ),
        out_specs=P(None, ("grp", "beam"), None, None),
        check_vma=False,
    )
```

time: 235 us -> 75.2 us (0.32)
  waiting for transfers between devices: 156 us -> 0 us
  Pallas kernels: 0 us -> 60.9 us
  blocking collectives: 30.6 us -> 0 us
  between operations: 14.2 us -> 0.01 us
  other arithmetic: 10.8 us -> 0.84 us
  matrix products: 18 us -> 12.7 us
  local copies, waits for them, and re-layouts: 5.6 us -> 0.69 us
    psum x1 -> x0, waiting for transfers between devices: 113 us -> none  [body(): full_re, full_im = lax.psum((wave_re, wave_im), 'beam')]
    pallas_call x0 -> x1, Pallas kernels: none -> 60.9 us  [body(): pl.pallas_call(functools.partial(wave_kernel, n, local, tile_count, pixel...]
    all_gather x1 -> x0, waiting for transfers between devices: 42.7 us -> none  [body(): whole_targets = lax.all_gather(target, 'beam', axis=1, tiled=True)]
    all_gather x1 -> x0, blocking collectives: 23.4 us -> none  [body(): lax.all_gather(probe_shift, 'beam', axis=0, tiled=True)]
    unnamed x1 -> x0, blocking collectives: 7.17 us -> none
    another operation x1 -> x0, other arithmetic: 6.75 us -> none  [body(): s_grad = jnp.stack([g_re, g_im]).reshape(2, local, tile_count, pixels)]
    dot_general x4 -> x1, matrix products: 18 us -> 12.7 us  [body(): lax.dot_general(left, res, (((0,), (0,)), ((), ())), preferred_element_ty...]
    unnamed x8 -> x0, local copies, waits for them, and re-layouts: 4.7 us -> none
  transfers between devices with their start and end apart: 2 -> 0, of which waited for: 2 -> 0; matrix products, arithmetic and copies ran while one was open for 0% -> 0% of each run, Pallas kernels for 0% -> 0%
where the time goes in v1:
time: 75.2 us; the launch traced here: 75.1 us
  Pallas kernels  60.9 us (81%)
  matrix products  12.7 us (17%)
  other arithmetic  0.84 us (1%)
    pallas_call x1, Pallas kernels, body(): pl.pallas_call(functools.partial(wave_kernel, n, local, tile_count, pixel...  60.9 us
    dot_general x1, matrix products, body(): lax.dot_general(left, res, (((0,), (0,)), ((), ())), preferred_element_ty...  12.7 us

profile of v1, /device:TPU:0, one launch (start us, length us, event | category | flops | bytes accessed | tf_op | source)
XLA Modules:
  0.0 75.1 jit_solution(14298841164347531766)
XLA Ops:
  0.0 0.8 %add_add_fusion = s32[16,4]{0,1:T(4,128)S(1)} fusion(s32[8,1]{0,1:T(1,128)} %bitcast.9, s32[8,1]{0,1:T(1,128)} %bitcast.10, s32[8,2]{0,1:T(2,128)} %param.8), kind=kLoop, calls=%fused_computation.1 | loop fusion | flops 320 | bytes 384 | tf_op jit(solution)/shard_map/concatenate | solution.py:188
  0.8 0.1 copy.10
  0.9 0.6 pad.4.par_ref
  1.5 60.9 %shard_map.64 = (bf16[256,4096]{1,0:T(8,128)(2,1)}, bf16[256,2048]{1,0:T(8,128)(2,1)}) custom-call(s32[16,128]{1,0:T(8,128)} %pad.4.par_ref, f32[2,64]{1,0:T(2,128)} %weight_ref.1, bf16[16,4096]{1,0:T(8,128)(2,1)} %bitcast.8, bf16[2048,4096]{1,0:T(8,128)(2,1)} %bitcast.7), custom_call_target="tpu_custom_call" | custom-call | tf_op jit(solution)/shard_map/pallas_call | solution.py:190
  62.4 12.7 %convolution_convert_fusion = bf16[2048,4096]{1,0:T(8,128)(2,1)} fusion(bf16[256,2048]{1,0:T(8,128)(2,1)} %get-tuple-element.7, bf16[256,4096]{1,0:T(8,128)(2,1)} %get-tuple-element.8), kind=kOutput, calls=%fused_computation | convolution fusion | flops 4303355904 | bytes 19922944 | tf_op jit(solution)/shard_map/dot_general | solution.py:214

commit v2 on v1

--- a/solution.py
+++ b/solution.py
@@ -12,12 +12,23 @@
 GRID = 192
 TILE_SIDE = 4
 TWO_PI = 2.0 * math.pi
-CHUNKS = 4
+CHUNKS = 8
+SWAP = False
+GAP_NEAR = 2
+GAP_FAR = 3
 MATMUL_COLUMNS = 512
 
 
 def stage_strides(n):
     return [2**k for k in range(n.bit_length() - 1)]
+
+
+def orders(n):
+    strides = stage_strides(n)
+    other = list(strides)
+    if SWAP and len(other) > 2:
+        other[1], other[2] = other[2], other[1]
+    return strides, other
 
 
 def place(me, strides, unit, upto):
@@ -29,10 +40,10 @@
 
 
 def wave_kernel(
-    n, local, tile_count, pixels, strides,
+    n, local, tile_count, pixels, strides, other,
     par_ref, weight_ref, target_ref, s_ref,
     res_ref, left_ref,
-    pars, s_vmem, acc, sbuf, rbuf,
+    pars, s_vmem, acc, sbuf, rbuf, mixed_left, mixed_res,
     par_send, par_recv, s_sem, send_sem, recv_sem,
 ):
     levels = len(strides)
@@ -42,8 +53,13 @@
     width = local * tile_count
     wide = pixels // CHUNKS
 
-    def partner(k):
-        return me + (1 - 2 * ((me // strides[k]) % 2)) * strides[k]
+    def order(c):
+        return other if c % 2 else strides
+
+    moves = [(place(i, other, unit, levels), place(i, strides, unit, levels)) for i in range(n)]
+
+    def partner(stride):
+        return me + (1 - 2 * ((me // stride) % 2)) * stride
 
     def columns(c):
         return pl.ds(c * wide, wide)
@@ -55,33 +71,38 @@
         loads.append(load)
 
     barrier = pltpu.get_barrier_semaphore()
-    for k in range(levels):
-        pl.semaphore_signal(barrier, inc=1, device_id={"beam": partner(k)}, device_id_type=pl.DeviceIdType.MESH)
-    pl.semaphore_wait(barrier, levels)
+    for ahead in range(1, n):
+        pl.semaphore_signal(
+            barrier, inc=1, device_id={"beam": lax.rem(me + ahead, n)}, device_id_type=pl.DeviceIdType.MESH
+        )
+    pl.semaphore_wait(barrier, n - 1)
 
     sent = []
 
-    def send(source, target, send_semaphore, recv_semaphore, k):
+    def send(source, target, send_semaphore, recv_semaphore, peer):
         copy = pltpu.make_async_remote_copy(
             src_ref=source,
             dst_ref=target,
             send_sem=send_semaphore,
             recv_sem=recv_semaphore,
-            device_id={"beam": partner(k)},
+            device_id={"beam": peer},
             device_id_type=pl.DeviceIdType.MESH,
         )
         copy.start()
         sent.append(copy)
         return copy
 
-    def mine(k):
+    def mine(k, steps=strides):
         size = unit * 2 ** (levels - k)
-        return pl.ds(pl.multiple_of(place(me, strides, unit, k), size), size)
+        return pl.ds(pl.multiple_of(place(me, steps, unit, k), size), size)
 
     pars[mine(levels), :] = par_ref[...]
-    for k in reversed(range(levels)):
-        held = pars.at[mine(k + 1), :]
-        send(held, held, par_send.at[k], par_recv.at[k], k).wait_recv()
+    asked = [
+        send(par_ref, pars.at[mine(levels), :], par_send.at[ahead - 1], par_recv.at[ahead - 1], lax.rem(me + ahead, n))
+        for ahead in range(1, n)
+    ]
+    for copy in asked:
+        copy.wait_recv()
 
     half = SIDE // 2
     beam = me * local + lax.broadcasted_iota(jnp.int32, (1, local), 1)
@@ -112,53 +133,74 @@
         full = jnp.dot(part, spread, preferred_element_type=jnp.float32)
         left_ref[:, at : at + width] = jnp.where(chosen, full, 0.0).astype(jnp.bfloat16)
 
+    if other != strides:
+        for at, old in moves:
+            mixed_left[at : at + unit, :] = left_ref[old : old + unit, :]
+
+    def left_of(c):
+        return left_ref if order(c) == strides else mixed_left
+
+    def res_of(c):
+        return res_ref if order(c) == strides else mixed_res
+
     narrow = min(MATMUL_COLUMNS, wide)
 
     def multiply(c):
         def tile(i, carry):
             at = pl.ds(pl.multiple_of(c * wide + i * narrow, narrow), narrow)
-            acc[:, at] = jnp.dot(left_ref[...], s_vmem[:, at], preferred_element_type=jnp.float32)
+            acc[:, at] = jnp.dot(left_of(c)[...], s_vmem[:, at], preferred_element_type=jnp.float32)
             return carry
 
         lax.fori_loop(0, wide // narrow, tile, 0)
 
-    def scatter_rows(k):
+    def scatter_rows(c, k):
         size = rows // 2 ** (k + 1)
-        base = place(me, strides, unit, k)
-        bit = (me // strides[k]) % 2
+        base = place(me, order(c), unit, k)
+        bit = (me // order(c)[k]) % 2
         keep = pl.ds(pl.multiple_of(base + bit * size, size), size)
         give = pl.ds(pl.multiple_of(base + (1 - bit) * size, size), size)
         slot = pl.ds(rows - 2 * size, size)
         return keep, give, slot
 
     def start_scatter(c, k):
-        _, give, slot = scatter_rows(k)
+        _, give, slot = scatter_rows(c, k)
         sbuf[slot, columns(c)] = acc[give, columns(c)].astype(jnp.bfloat16)
         return send(
-            sbuf.at[slot, columns(c)], rbuf.at[slot, columns(c)], send_sem.at[c, k], recv_sem.at[c, k], k
+            sbuf.at[slot, columns(c)],
+            rbuf.at[slot, columns(c)],
+            send_sem.at[c, k],
+            recv_sem.at[c, k],
+            partner(order(c)[k]),
         )
 
     def end_scatter(c, k):
-        keep, _, slot = scatter_rows(k)
+        keep, _, slot = scatter_rows(c, k)
         acc[keep, columns(c)] += rbuf[slot, columns(c)].astype(jnp.float32)
 
     def residual(c):
-        own = mine(levels)
+        own = mine(levels, order(c))
         scale = jnp.exp2(par_ref[:, 3:4].astype(jnp.float32))
         goal = target_ref[:, columns(c)].astype(jnp.float32) * scale
-        res_ref[own, columns(c)] = (acc[own, columns(c)] - goal).astype(jnp.bfloat16)
+        res_of(c)[own, columns(c)] = (acc[own, columns(c)] - goal).astype(jnp.bfloat16)
 
     def start_gather(c, k):
-        held = res_ref.at[mine(k + 1), columns(c)]
+        held = res_of(c).at[mine(k + 1, order(c)), columns(c)]
         at = 2 * levels - 1 - k
-        return send(held, held, send_sem.at[c, at], recv_sem.at[c, at], k)
+        return send(held, held, send_sem.at[c, at], recv_sem.at[c, at], partner(order(c)[k]))
+
+    def slots(c):
+        hops = order(c) + order(c)[::-1]
+        taken = [0]
+        for stride in hops:
+            taken.append(taken[-1] + (GAP_NEAR if stride == 1 else GAP_FAR))
+        return taken
 
     flight = {}
-    for time in range(CHUNKS + 2 * levels):
+    for time in range(CHUNKS + slots(0)[-1]):
         for c in range(CHUNKS):
-            at = time - c
-            if at < 0 or at > 2 * levels:
+            if time - c not in slots(c):
                 continue
+            at = slots(c).index(time - c)
             if at == 0:
                 loads[c].wait()
                 multiply(c)
@@ -172,14 +214,25 @@
                 if at == levels:
                     residual(c)
                 flight[c] = start_gather(c, 2 * levels - 1 - at)
+    for c in range(CHUNKS):
+        if order(c) != strides:
+            for at, old in moves:
+                res_ref[old : old + unit, columns(c)] = mixed_res[at : at + unit, columns(c)]
     for copy in sent:
         copy.wait_send()
+
+
+def grad_kernel(left_ref, res_ref, out_ref):
+    dims = (((0,), (0,)), ((), ()))
+    out_ref[...] = lax.dot_general(left_ref[...], res_ref[...], dims, preferred_element_type=jnp.float32).astype(
+        out_ref.dtype
+    )
 
 
 def body(n, s_matrix, beam_weight, probe_shift, probe_cutoff, target, target_exp):
     _, local, tile_count, pixels = s_matrix.shape
     probes = probe_shift.shape[0]
-    strides = stage_strides(n)
+    strides, other = orders(n)
     levels = len(strides)
     unit = 2 * probes
     rows = n * unit
@@ -188,7 +241,7 @@
     pars = jnp.pad(jnp.concatenate([pars, pars], axis=0), ((0, 0), (0, 124)))
     vmem = pl.BlockSpec(memory_space=pltpu.VMEM)
     res, left = pl.pallas_call(
-        functools.partial(wave_kernel, n, local, tile_count, pixels, strides),
+        functools.partial(wave_kernel, n, local, tile_count, pixels, strides, other),
         out_shape=(
             jax.ShapeDtypeStruct((rows, pixels), jnp.bfloat16),
             jax.ShapeDtypeStruct((rows, 2 * width), jnp.bfloat16),
@@ -201,8 +254,10 @@
             pltpu.VMEM((rows, pixels), jnp.float32),
             pltpu.VMEM((rows, pixels), jnp.bfloat16),
             pltpu.VMEM((rows, pixels), jnp.bfloat16),
-            pltpu.SemaphoreType.DMA((levels,)),
-            pltpu.SemaphoreType.DMA((levels,)),
+            pltpu.VMEM((rows, 2 * width), jnp.bfloat16),
+            pltpu.VMEM((rows, pixels), jnp.bfloat16),
+            pltpu.SemaphoreType.DMA((n - 1,)),
+            pltpu.SemaphoreType.DMA((n - 1,)),
             pltpu.SemaphoreType.DMA((CHUNKS,)),
             pltpu.SemaphoreType.DMA((CHUNKS, 2 * levels)),
             pltpu.SemaphoreType.DMA((CHUNKS, 2 * levels)),
@@ -211,8 +266,19 @@
             collective_id=0, has_side_effects=True, vmem_limit_bytes=60 * 2**20
         ),
     )(pars, beam_weight, target.reshape(unit, pixels), s_matrix.reshape(2 * width, pixels))
-    grad = lax.dot_general(left, res, (((0,), (0,)), ((), ())), preferred_element_type=jnp.float32)
-    return grad.astype(jnp.bfloat16).reshape(2, local, tile_count, pixels)
+    tall = min(256, width)
+    grad = pl.pallas_call(
+        grad_kernel,
+        grid=(2 * width // tall,),
+        out_shape=jax.ShapeDtypeStruct((2 * width, pixels), jnp.bfloat16),
+        in_specs=[
+            pl.BlockSpec((rows, tall), lambda i: (0, i)),
+            pl.BlockSpec((rows, pixels), lambda i: (0, 0)),
+        ],
+        out_specs=pl.BlockSpec((tall, pixels), lambda i: (i, 0)),
+        compiler_params=pltpu.CompilerParams(vmem_limit_bytes=60 * 2**20),
+    )(left, res)
+    return grad.reshape(2, local, tile_count, pixels)
 
 
 def solution(mesh):

time: 75.2 us -> 62.8 us (0.84)
  matrix products: 12.7 us -> 0 us
    dot_general x1 -> x0, matrix products: 12.7 us -> none  [body(): lax.dot_general(left, res, (((0,), (0,)), ((), ())), preferred_element_ty...]
    pallas_call x0 -> x1, Pallas kernels: none -> 10.9 us  [body(): pl.pallas_call(grad_kernel, grid=(2 * width // tall,), out_shape=jax.Shap...]
    pallas_call x1, Pallas kernels: 60.9 us -> 50.1 us  [body(): pl.pallas_call(functools.partial(wave_kernel, n, local, tile_count, pixel...]
where the time goes in v2:
time: 62.8 us; the launch traced here: 62.5 us
  Pallas kernels  61 us (97%)
  other arithmetic  0.84 us (1%)
  local copies, waits for them, and re-layouts  0.69 us (1%)
    pallas_call x1, Pallas kernels, body(): pl.pallas_call(functools.partial(wave_kernel, n, local, tile_count, pixel...  50.1 us
    pallas_call x1, Pallas kernels, body(): pl.pallas_call(grad_kernel, grid=(2 * width // tall,), out_shape=jax.Shap...  10.9 us

profile of v2, /device:TPU:0, one launch (start us, length us, event | category | flops | bytes accessed | tf_op | source)
XLA Modules:
  0.0 62.5 jit_solution(17519756801664710634)
XLA Ops:
  0.0 0.8 %add_add_fusion = s32[16,4]{0,1:T(4,128)S(1)} fusion(s32[8,1]{0,1:T(1,128)} %bitcast.7, s32[8,1]{0,1:T(1,128)} %bitcast.8, s32[8,2]{0,1:T(2,128)} %param.8), kind=kLoop, calls=%fused_computation | loop fusion | flops 320 | bytes 384 | tf_op jit(solution)/shard_map/concatenate | solution.py:241
  0.8 0.1 copy.10
  0.9 0.6 pad.4.par_ref
  1.5 50.1 %shard_map.64 = (bf16[256,4096]{1,0:T(8,128)(2,1)}, bf16[256,2048]{1,0:T(8,128)(2,1)}) custom-call(s32[16,128]{1,0:T(8,128)} %pad.4.par_ref, f32[2,64]{1,0:T(2,128)} %weight_ref.1, bf16[16,4096]{1,0:T(8,128)(2,1)} %bitcast.6, bf16[2048,4096]{1,0:T(8,128)(2,1)} %bitcast.5), custom_call_target="tpu_custom_call" | custom-call | tf_op jit(solution)/shard_map/pallas_call | solution.py:243
  51.6 10.9 %shard_map.65 = bf16[2048,4096]{1,0:T(8,128)(2,1)} custom-call(bf16[256,2048]{1,0:T(8,128)(2,1)} %get-tuple-element.7.left_ref, bf16[256,4096]{1,0:T(8,128)(2,1)} %get-tuple-element.8.res_ref), custom_call_target="tpu_custom_call" | custom-call | tf_op jit(solution)/shard_map/pallas_call | solution.py:270

commit v3 on v2

--- a/solution.py
+++ b/solution.py
@@ -13,9 +13,9 @@
 TILE_SIDE = 4
 TWO_PI = 2.0 * math.pi
 CHUNKS = 8
-SWAP = False
+SWAP = True
 GAP_NEAR = 2
-GAP_FAR = 3
+GAP_FAR = 4
 MATMUL_COLUMNS = 512
 
 
@@ -266,7 +266,7 @@
             collective_id=0, has_side_effects=True, vmem_limit_bytes=60 * 2**20
         ),
     )(pars, beam_weight, target.reshape(unit, pixels), s_matrix.reshape(2 * width, pixels))
-    tall = min(256, width)
+    tall = min(512, width)
     grad = pl.pallas_call(
         grad_kernel,
         grid=(2 * width // tall,),

time: 62.8 us -> 60.7 us (0.967)
  Pallas kernels: 61 us -> 58.9 us
    pallas_call x1, Pallas kernels: 10.9 us -> 9.67 us  [body(): pl.pallas_call(grad_kernel, grid=(2 * width // tall,), out_shape=jax.Shap...]
    pallas_call x1, Pallas kernels: 50.1 us -> 49.2 us  [body(): pl.pallas_call(functools.partial(wave_kernel, n, local, tile_count, pixel...]
where the time goes in v3:
time: 60.7 us; the launch traced here: 60.4 us
  Pallas kernels  58.9 us (97%)
  other arithmetic  0.84 us (1%)
  local copies, waits for them, and re-layouts  0.69 us (1%)
    pallas_call x1, Pallas kernels, body(): pl.pallas_call(functools.partial(wave_kernel, n, local, tile_count, pixel...  49.2 us
    pallas_call x1, Pallas kernels, body(): pl.pallas_call(grad_kernel, grid=(2 * width // tall,), out_shape=jax.Shap...  9.67 us

profile of v3, /device:TPU:0, one launch (start us, length us, event | category | flops | bytes accessed | tf_op | source)
XLA Modules:
  0.0 60.4 jit_solution(6843019539188443384)
XLA Ops:
  0.0 0.8 %add_add_fusion = s32[16,4]{0,1:T(4,128)S(1)} fusion(s32[8,1]{0,1:T(1,128)} %bitcast.7, s32[8,1]{0,1:T(1,128)} %bitcast.8, s32[8,2]{0,1:T(2,128)} %param.8), kind=kLoop, calls=%fused_computation | loop fusion | flops 320 | bytes 384 | tf_op jit(solution)/shard_map/concatenate | solution.py:241
  0.8 0.1 copy.10
  0.9 0.6 %pad.4.par_ref = s32[16,128]{1,0:T(8,128)} pad(s32[16,4]{1,0:T(8,128)S(1)} %copy.10, s32[]{:T(128)} %constant.0.clone.1), padding=0_0x0_124 | pad | bytes 8452 | tf_op jit(solution)/shard_map/jit(_pad)/pad | solution.py:241
  1.5 49.2 %shard_map.64 = (bf16[256,4096]{1,0:T(8,128)(2,1)}, bf16[256,2048]{1,0:T(8,128)(2,1)}) custom-call(s32[16,128]{1,0:T(8,128)} %pad.4.par_ref, f32[2,64]{1,0:T(2,128)} %weight_ref.1, bf16[16,4096]{1,0:T(8,128)(2,1)} %bitcast.6, bf16[2048,4096]{1,0:T(8,128)(2,1)} %bitcast.5), custom_call_target="tpu_custom_call" | custom-call | tf_op jit(solution)/shard_map/pallas_call | solution.py:243
  50.7 9.7 %shard_map.65 = bf16[2048,4096]{1,0:T(8,128)(2,1)} custom-call(bf16[256,2048]{1,0:T(8,128)(2,1)} %get-tuple-element.7.left_ref, bf16[256,4096]{1,0:T(8,128)(2,1)} %get-tuple-element.8.res_ref), custom_call_target="tpu_custom_call" | custom-call | tf_op jit(solution)/shard_map/pallas_call | solution.py:270
